TPU v7x, 256 devices: a whole 4x4x8 slice. The times are simulated.
256 devices in a mesh: req: 16 (over y, z_lo, core), blk: 16 (over z_hi, x).
Axes of the slice: x: 4, y: 4, z: 8 (z_hi: 4, z_lo: 2; z = z_hi * 2 + z_lo), core: 2. Of those that a mesh axis runs over, the one named last changes fastest.
Arguments:
- queries: bfloat16 [2048, 8192], P('req', 'blk'), may hold values from -120 to 120
- suffix_key_value: bfloat16 [2048, 8, 256], P('req'), may hold values from -6 to 6
- residual: bfloat16 [2048, 8192], P('req', 'blk'), may hold values from -10 to 10
- gain: float32 [8192], P('blk'), may hold values from 0.1 to 1.9
- gate_up: bfloat16 [8192, 2, 14336], P('blk', None, 'req'), may hold values from -0.0625 to 0.0625
- prefix_cache_slots: bfloat16 [128, 128, 8, 256], P('req'), may hold values from -6 to 6
- prefix_page_slots: int32 [128], replicated, may hold values from 0 to 127, each once
- lengths: int32 [16, 4], replicated, may hold values from 1 to 64, 128 in all within a row
- counts: int32 [16], replicated, may hold values from 1 to 128, as said below
Outputs:
- hidden: bfloat16 [2048, 14336], P('blk', 'req')
- suffix_cache: bfloat16 [2048, 2048], P('req', 'blk')
Inputs may be any that keep to these rules, and one draw needn't show every extreme that they name: `prefix_page_slots`: slot s of prefix_cache_slots lies on index s // 8 of req; every slot holds exactly one page. Each group's lengths sum to 128, and each group has one request of exactly 64 tokens. `counts`: some group reads all 128 pages.
All inputs are finite; a program needn't handle non-finite values.
Results may differ from a plain program's by a relative error of at most 0.034.
Values may be sent and summed in bfloat16 or wider, within the bound.
A program may use at most 256 MiB of HBM per device.

v0:
```python
import math

import jax
import jax.numpy as jnp
from jax import lax
from jax.experimental import pallas as pl
from jax.experimental.pallas import tpu as pltpu
from jax.sharding import PartitionSpec as P
import numpy as np

D = 8192

MESH = pl.DeviceIdType.MESH

NEGATIVE = -1e30
EPSILON = 1e-05
ROPE_BASE = 500000.0


def inverse_frequencies(half_dim):
    exponent = np.float32(-math.log(ROPE_BASE)) * np.arange(half_dim, dtype=np.float32)
    exponent = exponent * np.float32(2.0) / np.float32(2 * half_dim)
    inverse = np.exp(exponent.astype(np.float64)).astype(np.float32)
    return np.concatenate([inverse, inverse])[None, :]


def remote(src, dst, send_sem, recv_sem, req, blk):
    return pltpu.make_async_remote_copy(
        src_ref=src,
        dst_ref=dst,
        send_sem=send_sem,
        recv_sem=recv_sem,
        device_id=(req, blk),
        device_id_type=MESH,
    )


def place():
    req, blk = lax.axis_index("req"), lax.axis_index("blk")
    y, zl, core = req // 4, (req // 2) % 2, req % 2
    return req, blk, y, zl, core, blk // 4, blk % 4


def weight_pieces(w_ref, w_all, chunk):
    half = w_ref.shape[0] // 2

    def own(part):
        return w_ref.at[pl.ds(part * half, half), chunk]

    def slot(source, part):
        return w_all.at[source, pl.ds(part * half, half), chunk]

    return own, slot


def weight_sends(w_ref, w_all, send, recv, q, chunk):
    req, blk, y, zl, core, zh, x = place()
    own, slot = weight_pieces(w_ref, w_all, chunk)
    return [
        remote(
            own(part),
            slot(x, part),
            send.at[j, q],
            recv.at[x, part, q],
            req,
            zh * 4 + (x + 4 + step) % 4,
        )
        for j, (step, part) in enumerate(((1, 0), (-1, 1), (1, 1), (-1, 0)))
    ]


def weight_relays(w_ref, w_all, send, recv, q, chunk):
    req, blk, y, zl, core, zh, x = place()
    own, slot = weight_pieces(w_ref, w_all, chunk)
    out = []
    for j, (step, part) in enumerate(((1, 0), (-1, 1))):
        source = (x + 4 - step) % 4
        piece = slot(source, part)
        to_blk = zh * 4 + (x + 4 + step) % 4
        out.append(remote(piece, piece, send.at[4 + j, q], recv.at[source, part, q], req, to_blk))
    return out


def weight_wait(w_ref, w_all, send, recv, q, chunk, source, part):
    req, blk, y, zl, core, zh, x = place()
    piece = weight_pieces(w_ref, w_all, chunk)[1](source, part)
    to_blk = zh * 4 + (x + 1) % 4
    remote(piece, piece, send.at[0, q], recv.at[source, part, q], req, to_blk).wait_recv()


def spread_features(
    u_ref, a_all, x_send, z_send, y_send, on_send, core_send, recv, after_hop
):
    req, blk, y, zl, core, zh, x = place()
    target = zl * 2 + core
    home = core == x % 2
    root = x == target
    over_z = y * 4 + (1 - zl) * 2 + core
    sibling = y * 4 + zl * 2 + (1 - core)
    up, down = (y + 1) % 4, (y + 3) % 4
    far = (y + 2) % 4
    req_up, req_down = up * 4 + zl * 2 + core, down * 4 + zl * 2 + core

    def block_copy(yy, xx, send, to_req, to_blk):
        piece = a_all.at[yy, xx]
        return remote(piece, piece, send, recv.at[yy, xx], to_req, to_blk)

    hop = remote(u_ref, a_all.at[y, x], x_send, recv.at[y, x], req, zh * 4 + target)
    keep = pltpu.make_async_copy(u_ref, a_all.at[y, x], recv.at[y, x])

    @pl.when(root)
    def _():
        keep.start()

    @pl.when(jnp.logical_not(root))
    def _():
        hop.start()

    after_hop()

    def to_core(yy, xx):
        return block_copy(yy, xx, core_send.at[yy, xx], sibling, blk)

    def to_z(xx):
        return block_copy(y, xx, z_send.at[xx], over_z, blk)

    def to_y(xx, way):
        return block_copy(y, xx, y_send.at[xx, way], (req_up, req_down)[way], blk)

    def onward(xx, way):
        return block_copy((down, up)[way], xx, on_send.at[xx], (req_up, req_down)[way], blk)

    def arrived(yy, xx):
        block_copy(yy, xx, x_send, over_z, blk).wait_recv()

    @pl.when(home)
    def _():
        def own(xx, carry):
            @pl.when(root & (xx == x))
            def _():
                keep.wait()

            @pl.when(jnp.logical_not(root & (xx == x)))
            def _():
                arrived(y, xx)

            @pl.when(root)
            def _():
                to_z(xx).start()

            to_y(xx, 0).start()
            to_y(xx, 1).start()
            to_core(y, xx).start()
            return carry

        lax.fori_loop(0, 4, own, 0)

        def near(xx, carry):
            arrived(down, xx)

            @pl.when(xx < 2)
            def _():
                onward(xx, 0).start()

            to_core(down, xx).start()
            arrived(up, xx)

            @pl.when(xx >= 2)
            def _():
                onward(xx, 1).start()

            to_core(up, xx).start()
            return carry

        lax.fori_loop(0, 4, near, 0)

        def last(xx, carry):
            arrived(far, xx)
            to_core(far, xx).start()
            return carry

        lax.fori_loop(0, 4, last, 0)

    @pl.when(jnp.logical_not(home))
    def _():
        def take(i, carry):
            arrived(i // 4, i % 4)
            return carry

        lax.fori_loop(0, 16, take, 0)

    def drain():
        @pl.when(jnp.logical_not(root))
        def _():
            hop.wait_send()

        @pl.when(home)
        def _():
            def step(xx, carry):
                @pl.when(root)
                def _():
                    to_z(xx).wait_send()

                to_y(xx, 0).wait_send()
                to_y(xx, 1).wait_send()

                @pl.when(xx < 2)
                def _():
                    onward(xx, 0).wait_send()

                @pl.when(xx >= 2)
                def _():
                    onward(xx, 1).wait_send()

                return carry

            lax.fori_loop(0, 4, step, 0)

            def core_step(i, carry):
                to_core(i // 4, i % 4).wait_send()
                return carry

            lax.fori_loop(0, 16, core_step, 0)

    return drain


def group_at(j):
    return j + j // 2 - 2 * (j // 3)


def layer_kernel(
    lengths_ref,
    counts_ref,
    q_ref,
    inverse_ref,
    page_slots_ref,
    suffix_ref,
    residual_ref,
    gain_ref,
    cache_ref,
    w_ref,
    hidden_ref,
    updated_ref,
    slab,
    pages_ref,
    fresh_ref,
    hide,
    q_all,
    kv_all,
    values_t,
    scores,
    probs,
    part_out,
    stat_out,
    part_in,
    stat_in,
    held_part,
    held_stat,
    u_ref,
    w_all,
    a_all,
    product,
    relay,
    final,
    own_sum,
    square_out,
    square_in,
    query_send,
    query_recv,
    page_send,
    page_recv,
    part_send,
    part_recv,
    stat_send,
    stat_recv,
    w_send,
    w_recv,
    w_local,
    x_send,
    z_send,
    y_send,
    on_send,
    core_send,
    a_recv,
    r_send,
    relay_recv,
    final_recv,
    q_send,
    q_recv,
    slab_recv,
):
    req, blk, y, zl, core, zh, x = place()
    tokens, features = q_ref.shape
    heads = features // 128
    keys_here = slab.shape[0]
    rows_all = heads * tokens
    width = hidden_ref.shape[1]
    sibling = y * 4 + zl * 2 + (1 - core)
    blk_up, blk_far, blk_down = [((zh + i) % 4) * 4 + x for i in (1, 2, 3)]
    turn = (1.0 / math.sqrt(128)) * math.log2(math.e)

    chunks_w = (pl.ds(0, width), pl.ds(width, width))
    over_z = y * 4 + (1 - zl) * 2 + core

    def ahead(j):
        return ((y + group_at(j)) % 4) * 4 + zl * 2 + core

    def behind(j):
        return ((y + 4 - group_at(j)) % 4) * 4 + zl * 2 + core

    barrier = pltpu.get_barrier_semaphore()
    peers = [(req, zh * 4 + (x + i) % 4) for i in (1, 2, 3)]
    peers += [(sibling, blk), (req, blk_up), (req, blk_far), (req, blk_down)]
    peers += [(over_z, blk)] + [(ahead(j), blk) for j in range(1, 4)]
    for peer in peers:
        pl.semaphore_signal(barrier, inc=1, device_id=peer, device_id_type=MESH)

    pieces = slab_recv.shape[0]
    keys_piece = keys_here // pieces
    slab_copies = [
        pltpu.make_async_copy(
            cache_ref.at[pl.ds(i * keys_piece, keys_piece)],
            slab.at[pl.ds(i * keys_piece, keys_piece)],
            slab_recv.at[i],
        )
        for i in range(pieces)
    ]
    for copy in slab_copies:
        copy.start()

    own_lengths = [lengths_ref[i, req] for i in range(3)]
    starts = [own_lengths[0], own_lengths[0] + own_lengths[1]]
    starts.append(starts[1] + own_lengths[2])
    down_rows = lax.broadcasted_iota(jnp.int32, (tokens, 128), 0)
    along = lax.broadcasted_iota(jnp.int32, (tokens, 128), 1)

    def begin_of(token):
        begin = jnp.zeros_like(token)
        for start in starts:
            begin = jnp.where(token >= start, start, begin)
        return begin

    begin = begin_of(down_rows)
    position = counts_ref[req] * 128 + (down_rows - begin)
    angle = position.astype(jnp.float32) * inverse_ref[...]
    cosines = jnp.cos(angle)
    sines = jnp.where(along < 64, -1.0, 1.0) * jnp.sin(angle)
    allowed = (begin == begin_of(along)) & (down_rows <= along)

    def turned(vector):
        return (vector * cosines + pltpu.roll(vector, 64, 1) * sines).astype(jnp.bfloat16)

    head = blk // 2
    chosen = lax.broadcasted_iota(jnp.int32, (1, 8, 256), 1) == head
    chosen = chosen.astype(jnp.bfloat16)

    def pick_head(block):
        block = block * chosen
        block = block[:, 0:4] + block[:, 4:8]
        block = block[:, 0:2] + block[:, 2:4]
        return block[:, 0] + block[:, 1]

    for h in range(heads):
        vector = q_ref[:, h * 128 : (h + 1) * 128].astype(jnp.float32)
        q_all[0, h * tokens : (h + 1) * tokens, :] = turned(vector)
    pl.semaphore_wait(barrier, len(peers))

    def part_of(r):
        return ((zl + r // 2) % 2) * 2 + (core + r % 2) % 2

    def page_piece(r, send, to_req):
        piece = kv_all.at[part_of(r)]
        return remote(piece, piece, page_send.at[send], page_recv.at[part_of(r)], to_req, blk)

    own_pages = kv_all.at[part_of(0)]
    page_copies = [
        remote(pages_ref, own_pages, page_send.at[i], page_recv.at[part_of(0)], to_req, blk)
        for i, to_req in enumerate((sibling, over_z))
    ]
    page_on = page_piece(2, 2, sibling)
    query_copies = [
        remote(q_all.at[0], q_all.at[j], query_send.at[j], query_recv.at[j], ahead(j), blk)
        for j in range(1, 4)
    ]
    sends = [weight_sends(w_ref, w_all, w_send, w_recv, q, chunks_w[q]) for q in range(2)]
    for copy in query_copies + sends[0]:
        copy.start()
    local = pltpu.make_async_copy(w_ref, w_all.at[x], w_local)
    local.start()
    for i, copy in enumerate(slab_copies):
        copy.wait()

        def pick(p, carry):
            rows = pl.ds(pl.multiple_of(i * keys_piece + p * 128, 128), 128)
            pages_ref[rows, :] = pick_head(slab[rows])
            return carry

        lax.fori_loop(0, keys_piece // 128, pick, 0)
    for copy in page_copies:
        copy.start()
    kv_all[part_of(0)] = pages_ref[...]

    suffix = pick_head(suffix_ref[...])
    fresh_ref[:, 0:128] = turned(suffix[:, 0:128].astype(jnp.float32))
    fresh_ref[:, 128:256] = suffix[:, 128:256]

    @pl.when(blk % 2 == 0)
    def _():
        updated_ref[...] = fresh_ref[:, 0:128]

    @pl.when(blk % 2 == 1)
    def _():
        updated_ref[...] = fresh_ref[:, 128:256]

    slots_here = 4 * keys_here // 128
    slot_ids = (req // 4) * slots_here + lax.broadcasted_iota(jnp.int32, (slots_here, 128), 0)
    page_ids = lax.broadcasted_iota(jnp.int32, (slots_here, 128), 1).astype(jnp.float32)
    match = page_slots_ref[...] == slot_ids
    page_of = jnp.sum(jnp.where(match, page_ids, 0.0), 1, keepdims=True)
    for j in range(4):
        seen = counts_ref[behind(j)].astype(jnp.float32)
        level = jnp.where(page_of < seen, 0.0, NEGATIVE)
        for part in range(4):
            rows = slice(part * slots_here // 4, (part + 1) * slots_here // 4)
            hide[j, part] = jnp.broadcast_to(level[rows], (slots_here // 4, rows_all))

    def fold(block, op):
        parts = [block[i * 8 : (i + 1) * 8] for i in range(block.shape[0] // 8)]
        while len(parts) > 1:
            parts = [op(a, b) for a, b in zip(parts[::2], parts[1::2])]
        return parts[0]

    def last_fold(rows, op):
        return op(rows, 0, keepdims=True)

    fresh_t = jnp.transpose(fresh_ref[:, 128:256].astype(jnp.float32)).astype(jnp.bfloat16)
    raw = lax.dot_general(
        fresh_ref[:, 0:128],
        q_all[0],
        (((1,), (1,)), ((), ())),
        preferred_element_type=jnp.float32,
    )
    mask = jnp.concatenate([allowed.astype(jnp.float32)] * heads, 1)
    raw = jnp.where(mask > 0, raw, NEGATIVE)
    suffix_max = last_fold(fold(raw, jnp.maximum), jnp.max)
    suffix_probs = jnp.exp2((raw - suffix_max) * turn)
    suffix_sum = last_fold(fold(suffix_probs, jnp.add), jnp.sum)
    suffix_part = jnp.dot(
        fresh_t, suffix_probs.astype(jnp.bfloat16), preferred_element_type=jnp.float32
    )

    def turn_values(r):
        for p in range(keys_here // 128):
            block = kv_all[part_of(r), p * 128 : (p + 1) * 128, 128:256].astype(jnp.float32)
            start = r * keys_here + p * 128
            values_t[:, start : start + 128] = jnp.transpose(block).astype(jnp.bfloat16)

    turn_values(0)
    page_piece(1, 2, sibling).wait_recv()
    turn_values(1)

    chunk = 512
    chunks = 2 * keys_here // chunk
    per_core = keys_here // chunk

    def score_chunk(c, j, a, top):
        part = part_of(2 * a + c // per_core)
        inside = c % per_core
        keys = kv_all[part, inside * chunk : (inside + 1) * chunk, 0:128]
        raw = lax.dot_general(
            keys, q_all[j], (((1,), (1,)), ((), ())), preferred_element_type=jnp.float32
        )
        scores[c * chunk : (c + 1) * chunk, :] = raw
        for p in range(chunk // 128):
            page = inside * (chunk // 128) + p
            folded = fold(raw[p * 128 : (p + 1) * 128], jnp.maximum)
            top = jnp.maximum(top, folded + hide[j, part, page : page + 1, :])
        return top

    def weigh_chunk(c, j, a, top, total, weighted):
        part = part_of(2 * a + c // per_core)
        for p in range(chunk // 128):
            page = (c % per_core) * (chunk // 128) + p
            rows = slice(c * chunk + p * 128, c * chunk + (p + 1) * 128)
            level = top - 4.0 * hide[j, part, page : page + 1, :]
            weights = jnp.exp2((scores[rows, :] - level) * turn)
            total = total + fold(weights, jnp.add)
            probs[rows, :] = weights.astype(jnp.bfloat16)
        columns = pl.ds(pl.multiple_of(a * 2 * keys_here + c * chunk, chunk), chunk)
        product_here = jnp.dot(
            values_t[:, columns],
            probs[c * chunk : (c + 1) * chunk, :],
            preferred_element_type=jnp.float32,
        )
        return total, product_here if weighted is None else weighted + product_here

    first_row = lax.broadcasted_iota(jnp.int32, (8, rows_all), 0) == 0

    def merge(j, top, total, weighted):
        other_top, other_sum = held_stat[j, 0:1, :], held_stat[j, 1:2, :]
        joint = jnp.maximum(top, other_top)
        here, there = jnp.exp2((top - joint) * turn), jnp.exp2((other_top - joint) * turn)
        return joint, total * here + other_sum * there, weighted * here + held_part[j] * there

    def part_copies(j):
        return (
            remote(
                part_out.at[j], part_in.at[j], part_send.at[j], part_recv.at[j], behind(j), blk
            ),
            remote(
                stat_out.at[j], stat_in.at[j], stat_send.at[j], stat_recv.at[j], behind(j), blk
            ),
        )

    def unit(u):
        v = u - 4
        later = jnp.where(v == 0, 3, jnp.where(v == 3, 0, v))
        return jnp.where(u < 4, u, later), jnp.where(u < 4, 0, 1)

    low = jnp.full((8, rows_all), NEGATIVE, jnp.float32)
    zero = jnp.zeros((8, rows_all), jnp.float32)

    relays = [weight_relays(w_ref, w_all, w_send, w_recv, q, chunks_w[q]) for q in range(2)]

    def relay_chunk(q):
        for (step, part), copy in zip(((1, 0), (-1, 1)), relays[q]):
            source = (x + 4 - step) % 4
            weight_wait(w_ref, w_all, w_send, w_recv, q, chunks_w[q], source, part)
            copy.start()

    def second_weights():
        for copy in sends[1]:
            copy.start()

    def unit_step(u, carry):
        j, a = unit(u)

        @pl.when(u == 7)
        def _():
            relay_chunk(0)

        @pl.when((u > 0) & (u < 4))
        def _():
            remote(
                q_all.at[0], q_all.at[j], query_send.at[1], query_recv.at[j], ahead(1), blk
            ).wait_recv()

        @pl.when(u == 3)
        def _():
            page_piece(2, 2, over_z).wait_recv()
            page_on.start()
            turn_values(2)

        @pl.when(u == 4)
        def _():
            page_piece(3, 2, sibling).wait_recv()
            turn_values(3)

        top, total, weighted = low, zero, None
        for c in range(chunks):
            top = score_chunk(c, j, a, top)
        top = last_fold(top, jnp.max)
        for c in range(chunks):
            total, weighted = weigh_chunk(c, j, a, top, total, weighted)
        total = last_fold(total, jnp.sum)

        @pl.when(u < 4)
        def _():
            held_part[j] = weighted
            held_stat[j] = jnp.where(first_row, top, total)

        @pl.when(u >= 4)
        def _():
            joint, joint_sum, joint_part = merge(j, top, total, weighted)

            @pl.when(u < 7)
            def _():
                part_out[j] = joint_part.astype(jnp.bfloat16)
                stat_out[j] = jnp.where(first_row, joint, joint_sum)
                for copy in part_copies(j):
                    copy.start()

            @pl.when(u == 7)
            def _():
                held_part[0] = joint_part
                held_stat[0] = jnp.where(first_row, joint, joint_sum)

        return carry

    lax.fori_loop(0, 8, unit_step, 0)

    order = (1, 2, 3)
    for j in order:
        part_copies(j)[1].wait_recv()
    tops = [stat_in[j, 0:1, :] for j in order]
    sums = [stat_in[j, 1:2, :] for j in order]
    own_top, own_total = held_stat[0, 0:1, :], held_stat[0, 1:2, :]
    joint = jnp.maximum(suffix_max, own_top)
    for row in tops:
        joint = jnp.maximum(joint, row)
    factor, own_factor = (jnp.exp2((row - joint) * turn) for row in (suffix_max, own_top))
    joint_sum = suffix_sum * factor + own_total * own_factor
    attended = suffix_part * factor + held_part[0] * own_factor
    for j, row, row_sum in zip(order, tops, sums):
        factor = jnp.exp2((row - joint) * turn)
        joint_sum = joint_sum + row_sum * factor
        part_copies(j)[0].wait_recv()
        attended = attended + part_in[j].astype(jnp.float32) * factor
    attended = attended / joint_sum

    squares_here = jnp.zeros((tokens, 128), jnp.float32)
    for h in range(heads):
        cols = slice(h * 128, (h + 1) * 128)
        own = jnp.transpose(attended[:, h * tokens : (h + 1) * tokens])
        stream = (residual_ref[:, cols].astype(jnp.float32) + own).astype(jnp.bfloat16)
        stream = stream.astype(jnp.float32)
        squares_here = squares_here + stream * stream
        u_ref[0:tokens, cols] = (stream * gain_ref[:, cols]).astype(jnp.bfloat16)
    square_row = jnp.sum(jnp.transpose(squares_here), 0, keepdims=True)
    high = square_row.astype(jnp.bfloat16)
    below = (square_row - high.astype(jnp.float32)).astype(jnp.bfloat16)
    u_ref[tokens : tokens + 16, 0:128] = jnp.broadcast_to(high, (16, 128))
    u_ref[tokens : tokens + 16, 128:256] = jnp.broadcast_to(below, (16, 128))
    u_ref[tokens : tokens + 16, 256:features] = jnp.zeros((16, features - 256), jnp.bfloat16)

    drain = spread_features(
        u_ref, a_all, x_send, z_send, y_send, on_send, core_send, a_recv, second_weights
    )

    def squares(zt, carry):
        total = jnp.zeros((8, 128), jnp.float32)
        for xx in range(4):
            rows = a_all[zt, xx, tokens : tokens + 16, 0:256].astype(jnp.float32)
            total = total + rows[0:8, 0:128] + rows[0:8, 128:256]
        square_out[zt] = total
        return carry

    lax.fori_loop(0, 4, squares, 0)
    square_copies = []
    for i in (1, 2, 3):
        there = (zh + i) % 4
        square_copies.append(
            remote(
                square_out.at[there],
                square_in.at[i - 1],
                q_send.at[i - 1],
                q_recv.at[i - 1],
                req,
                there * 4 + x,
            )
        )
    for copy in square_copies:
        copy.start()

    def multiply(zt, target, q):
        for start, size in ((0, 512), (512, width - 512)):
            cols = pl.ds(q * width + start, size)
            total = jnp.dot(
                a_all[zt, 0, 0:tokens, :], w_all[0, :, cols], preferred_element_type=jnp.float32
            )
            for xx in range(1, 4):
                total = total + jnp.dot(
                    a_all[zt, xx, 0:tokens, :],
                    w_all[xx, :, cols],
                    preferred_element_type=jnp.float32,
                )
            target[:, cols] = total.astype(target.dtype)

    half = tokens // 2
    top_rows, bottom_rows = pl.ds(0, half), pl.ds(half, half)

    def exchange(q):
        cols = chunks_w[q]

        def piece(i, slot, rows, target, recv, to_blk):
            source = product.at[slot, rows, cols]
            return remote(source, target, r_send.at[i, q], recv, req, to_blk)

        def landing(side, rows):
            return final.at[side, rows, cols]

        return (
            piece(0, 0, top_rows, relay.at[0, :, cols], relay_recv.at[0, q], blk_up),
            piece(1, 0, bottom_rows, relay.at[1, :, cols], relay_recv.at[1, q], blk_down),
            piece(2, 1, bottom_rows, landing(0, bottom_rows), final_recv.at[0, 1, q], blk_up),
            piece(3, 2, top_rows, landing(1, top_rows), final_recv.at[1, 0, q], blk_down),
            piece(4, 1, top_rows, landing(0, top_rows), final_recv.at[0, 0, q], blk_up),
            piece(5, 2, bottom_rows, landing(1, bottom_rows), final_recv.at[1, 1, q], blk_down),
        )

    exchanges = [exchange(0), exchange(1)]

    def wait_weights(q):
        for step, part in ((3, 0), (3, 1), (1, 0), (1, 1), (2, 0), (2, 1)):
            if (step, part) not in ((3, 0), (1, 1)):
                source = (x + step) % 4
                weight_wait(w_ref, w_all, w_send, w_recv, q, chunks_w[q], source, part)

    def add_relay(slot, rows, index, q):
        def tile(n, carry):
            cols = pl.ds(pl.multiple_of(q * width + n * 128, 128), 128)
            total = product[slot, rows, cols].astype(jnp.float32) + relay[index, :, cols].astype(
                jnp.float32
            )
            product[slot, rows, cols] = total.astype(jnp.bfloat16)
            return carry

        lax.fori_loop(0, width // 128, tile, 0)

    def send_far(q):
        wait_weights(q)
        multiply((zh + 2) % 4, product.at[0], q)
        exchanges[q][0].start()
        exchanges[q][1].start()

    def send_near(q):
        multiply((zh + 1) % 4, product.at[1], q)
        exchanges[q][2].start()
        multiply((zh + 3) % 4, product.at[2], q)
        exchanges[q][3].start()

    def send_sums(q):
        exchanges[q][0].wait_recv()
        add_relay(1, top_rows, 0, q)
        exchanges[q][4].start()
        exchanges[q][1].wait_recv()
        add_relay(2, bottom_rows, 1, q)
        exchanges[q][5].start()

    local.wait()
    send_far(0)
    send_near(0)
    relay_chunk(1)
    send_sums(0)
    send_far(1)
    send_near(1)
    send_sums(1)
    multiply(zh, own_sum, 0)
    multiply(zh, own_sum, 1)

    for copy in square_copies:
        copy.wait_recv()
    row = square_out[zh] + square_in[0] + square_in[1] + square_in[2]
    spread = jnp.broadcast_to(row[0:1, :], (tokens, tokens))
    diagonal = lax.broadcasted_iota(jnp.int32, (tokens, tokens), 0) == lax.broadcasted_iota(
        jnp.int32, (tokens, tokens), 1
    )
    square_sum = jnp.sum(jnp.where(diagonal, spread, 0.0), 1, keepdims=True)
    scale = jnp.broadcast_to(lax.rsqrt(square_sum / D + EPSILON), (tokens, 128))

    def finish(n, carry):
        def column_sum(start):
            cols = pl.ds(pl.multiple_of(start, 128), 128)
            total = own_sum[:, cols] + final[0, :, cols].astype(jnp.float32)
            return (total + final[1, :, cols].astype(jnp.float32)) * scale

        gate, up = column_sum(n * 128), column_sum(width + n * 128)
        value = gate / (1.0 + jnp.exp(-gate)) * up
        hidden_ref[:, pl.ds(pl.multiple_of(n * 128, 128), 128)] = value.astype(jnp.bfloat16)
        return carry

    for q in range(2):
        for copy in exchanges[q][2:]:
            copy.wait_recv()
    lax.fori_loop(0, width // 128, finish, 0)

    for copy in sends[0] + sends[1] + relays[0] + relays[1] + square_copies:
        copy.wait_send()
    for q in range(2):
        for copy in exchanges[q]:
            copy.wait_send()
    drain()
    for copy in query_copies + page_copies + [page_on]:
        copy.wait_send()
    for j in order:
        for copy in part_copies(j):
            copy.wait_send()


def layer(lengths, counts, q, page_slots, suffix, residual, gain, cache, weights):
    depth, wide = weights.shape
    tokens, features = q.shape
    rows_all = tokens * features // 128
    keys_here, _, lanes = cache.shape
    keys = 2 * keys_here
    groups = 4
    dma = pltpu.SemaphoreType.DMA
    bf16, f32 = jnp.bfloat16, jnp.float32
    vmem = pl.BlockSpec(memory_space=pltpu.VMEM)
    return pl.pallas_call(
        layer_kernel,
        out_shape=(
            jax.ShapeDtypeStruct((tokens, wide // 2), bf16),
            jax.ShapeDtypeStruct((tokens, 128), bf16),
        ),
        in_specs=[pl.BlockSpec(memory_space=pltpu.SMEM)] * 2
        + [vmem] * 6
        + [pl.BlockSpec(memory_space=pl.ANY)] * 2,
        out_specs=(vmem, vmem),
        scratch_shapes=[
            pltpu.VMEM(cache.shape, bf16),
            pltpu.VMEM((keys_here, lanes), bf16),
            pltpu.VMEM((tokens, lanes), bf16),
            pltpu.VMEM((groups, 4, keys_here // 128, rows_all), f32),
            pltpu.VMEM((groups, rows_all, 128), bf16),
            pltpu.VMEM((4, keys_here, lanes), bf16),
            pltpu.VMEM((128, 2 * keys), bf16),
            pltpu.VMEM((keys, rows_all), f32),
            pltpu.VMEM((keys, rows_all), bf16),
            pltpu.VMEM((groups, 128, rows_all), bf16),
            pltpu.VMEM((groups, 8, rows_all), f32),
            pltpu.VMEM((groups, 128, rows_all), bf16),
            pltpu.VMEM((groups, 8, rows_all), f32),
            pltpu.VMEM((groups, 128, rows_all), f32),
            pltpu.VMEM((groups, 8, rows_all), f32),
            pltpu.VMEM((tokens + 16, features), bf16),
            pltpu.VMEM((4, depth, wide), bf16),
            pltpu.VMEM((4, 4, tokens + 16, features), bf16),
            pltpu.VMEM((3, tokens, wide), bf16),
            pltpu.VMEM((2, tokens // 2, wide), bf16),
            pltpu.VMEM((2, tokens, wide), bf16),
            pltpu.VMEM((tokens, wide), f32),
            pltpu.VMEM((4, 8, 128), f32),
            pltpu.VMEM((3, 8, 128), f32),
            dma((groups,)),
            dma((groups,)),
            dma((3,)),
            dma((4,)),
            dma((groups,)),
            dma((groups,)),
            dma((groups,)),
            dma((groups,)),
            dma((6, 2)),
            dma((4, 2, 2)),
            dma,
            dma,
            dma((4,)),
            dma((4, 2)),
            dma((4,)),
            dma((4, 4)),
            dma((4, 4)),
            dma((6, 2)),
            dma((2, 2)),
            dma((2, 2, 2)),
            dma((3,)),
            dma((3,)),
            dma((4,)),
        ],
        compiler_params=pltpu.CompilerParams(collective_id=1, has_side_effects=True),
        name="layer",
    )(
        lengths,
        counts,
        q,
        jnp.asarray(inverse_frequencies(64)),
        page_slots,
        suffix,
        residual,
        gain,
        cache,
        weights,
    )


def on_device(
    queries,
    suffix_key_value,
    residual,
    gain,
    gate_up,
    prefix_cache_slots,
    prefix_page_slots,
    lengths,
    counts,
):
    slots, page_len, heads_kv, lanes = prefix_cache_slots.shape
    return layer(
        lengths.T,
        counts,
        queries,
        prefix_page_slots[None, :],
        suffix_key_value,
        residual,
        gain[None, :],
        prefix_cache_slots.reshape(slots * page_len, heads_kv, lanes),
        gate_up.reshape(gate_up.shape[0], 2 * gate_up.shape[2]),
    )


def solution(mesh):
    placed = (
        P("req", "blk"),
        P("req", None, None),
        P("req", "blk"),
        P("blk"),
        P("blk", None, "req"),
        P("req", None, None, None),
        P(),
        P(),
        P(),
    )
    return jax.shard_map(
        on_device,
        mesh=mesh,
        in_specs=placed,
        out_specs=(P("blk", "req"), P("req", "blk")),
        check_vma=False,
    )
```

profile of v0, /device:TPU:7, one launch (start us, length us, event | category | flops | bytes accessed | tf_op | source)
XLA Modules:
  0.0 105.2 jit_solution(16877183908221897402)
XLA Ops:
  0.6 3.0 %copy.12 = bf16[64,8,2,896]{3,1,2,0:T(8,128)(2,1)} copy(bf16[64,8,2,896]{3,2,1,0:T(2,128)(2,1)} %bitcast.8) | data formatting | bytes 3670016
  3.7 98.5 %layer.1 = (bf16[128,896]{1,0:T(8,128)(2,1)}, bf16[128,128]{1,0:T(8,128)(2,1)}) custom-call(s32[4,16]{1,0:T(4,128)} %bitcast.9, s32[16]{0:T(128)} %counts_ref.1, bf16[128,512]{1,0:T(8,128)(2,1)} %q_ref.1, f32[1,128]{1,0:T(1,128)} %constant.2.clone.inverse_ref, s32[1,128]{1,0:T(1,128)} %bitcast.11, bf16[128,8,256]{2,1,0:T(8,128)(2,1)} %suffix_ref.1, ...), custom_call_target="tpu_custom_call" | custom-call | tf_op jit(solution)/shard_map/layer/pallas_call | solution.py:791
  102.2 1.6 %copy.15 = bf16[128,896]{1,0:T(8,128)(2,1)} copy(bf16[128,896]{1,0:T(8,128)(2,1)} %get-tuple-element.4) | data formatting | bytes 458752
  103.9 1.4 %copy.16 = bf16[128,128]{1,0:T(8,128)(2,1)} copy(bf16[128,128]{1,0:T(8,128)(2,1)} %get-tuple-element.5) | data formatting | bytes 65536
where the time goes:
time: 105 us
  Pallas kernels  98.5 us (94%)
  local copies, waits for them, and re-layouts  6.06 us (6%)
    pallas_call x1, Pallas kernels, layer(): pl.pallas_call(layer_kernel, out_shape=(jax.ShapeDtypeStruct((tokens, wid...  98.5 us
    unnamed x3, local copies, waits for them, and re-layouts  6.06 us

commit v1 on v0

--- a/solution.py
+++ b/solution.py
@@ -101,128 +101,181 @@
     far = (y + 2) % 4
     req_up, req_down = up * 4 + zl * 2 + core, down * 4 + zl * 2 + core
 
-    def block_copy(yy, xx, send, to_req, to_blk):
-        piece = a_all.at[yy, xx]
-        return remote(piece, piece, send, recv.at[yy, xx], to_req, to_blk)
-
-    hop = remote(u_ref, a_all.at[y, x], x_send, recv.at[y, x], req, zh * 4 + target)
-    keep = pltpu.make_async_copy(u_ref, a_all.at[y, x], recv.at[y, x])
+    rows = u_ref.shape[0]
+    halves = (pl.ds(0, 64), pl.ds(64, rows - 64))
+    both = range(2)
+
+    def block_copy(yy, xx, h, send, to_req, to_blk):
+        piece = a_all.at[yy, xx, halves[h]]
+        return remote(piece, piece, send, recv.at[yy, xx, h], to_req, to_blk)
+
+    hops = [
+        remote(
+            u_ref.at[halves[h]],
+            a_all.at[y, x, halves[h]],
+            x_send.at[h],
+            recv.at[y, x, h],
+            req,
+            zh * 4 + target,
+        )
+        for h in both
+    ]
+    keeps = [
+        pltpu.make_async_copy(u_ref.at[halves[h]], a_all.at[y, x, halves[h]], recv.at[y, x, h])
+        for h in both
+    ]
 
     @pl.when(root)
     def _():
-        keep.start()
+        for keep in keeps:
+            keep.start()
 
     @pl.when(jnp.logical_not(root))
     def _():
-        hop.start()
+        for hop in hops:
+            hop.start()
 
     after_hop()
 
-    def to_core(yy, xx):
-        return block_copy(yy, xx, core_send.at[yy, xx], sibling, blk)
-
-    def to_z(xx):
-        return block_copy(y, xx, z_send.at[xx], over_z, blk)
-
-    def to_y(xx, way):
-        return block_copy(y, xx, y_send.at[xx, way], (req_up, req_down)[way], blk)
-
-    def onward(xx, way):
-        return block_copy((down, up)[way], xx, on_send.at[xx], (req_up, req_down)[way], blk)
-
-    def arrived(yy, xx):
-        block_copy(yy, xx, x_send, over_z, blk).wait_recv()
-
-    @pl.when(home)
-    def _():
-        def own(xx, carry):
-            @pl.when(root & (xx == x))
-            def _():
-                keep.wait()
-
-            @pl.when(jnp.logical_not(root & (xx == x)))
-            def _():
-                arrived(y, xx)
-
-            @pl.when(root)
-            def _():
-                to_z(xx).start()
-
-            to_y(xx, 0).start()
-            to_y(xx, 1).start()
-            to_core(y, xx).start()
-            return carry
-
-        lax.fori_loop(0, 4, own, 0)
-
-        def near(xx, carry):
-            arrived(down, xx)
-
-            @pl.when(xx < 2)
-            def _():
-                onward(xx, 0).start()
-
-            to_core(down, xx).start()
-            arrived(up, xx)
-
-            @pl.when(xx >= 2)
-            def _():
-                onward(xx, 1).start()
-
-            to_core(up, xx).start()
-            return carry
-
-        lax.fori_loop(0, 4, near, 0)
-
-        def last(xx, carry):
-            arrived(far, xx)
-            to_core(far, xx).start()
-            return carry
-
-        lax.fori_loop(0, 4, last, 0)
-
-    @pl.when(jnp.logical_not(home))
-    def _():
-        def take(i, carry):
-            arrived(i // 4, i % 4)
-            return carry
-
-        lax.fori_loop(0, 16, take, 0)
+    def to_core(yy, xx, h):
+        return block_copy(yy, xx, h, core_send.at[yy, xx, h], sibling, blk)
+
+    def to_z(xx, h):
+        return block_copy(y, xx, h, z_send.at[xx, h], over_z, blk)
+
+    def to_y(xx, h, way):
+        return block_copy(y, xx, h, y_send.at[xx, way, h], (req_up, req_down)[way], blk)
+
+    def onward(xx, h, way):
+        return block_copy((down, up)[way], xx, h, on_send.at[xx, h], (req_up, req_down)[way], blk)
+
+    def arrived(yy, xx, h):
+        block_copy(yy, xx, h, x_send.at[0], over_z, blk).wait_recv()
+
+    def nearest(i):
+        return (x + group_at(i)) % 4
+
+    def own_stage():
+        @pl.when(home)
+        def _():
+            def step(i, carry):
+                xx = nearest(i)
+
+                for h in both:
+
+                    @pl.when(root & (i == 0))
+                    def _():
+                        keeps[h].wait()
+
+                    @pl.when(jnp.logical_not(root & (i == 0)))
+                    def _():
+                        arrived(y, xx, h)
+
+                    to_y(xx, h, 0).start()
+                    to_y(xx, h, 1).start()
+
+                    @pl.when(root)
+                    def _():
+                        to_z(xx, h).start()
+
+                    to_core(y, xx, h).start()
+                return carry
+
+            lax.fori_loop(0, 4, step, 0)
+
+        take(y)
+
+    def near_stage():
+        @pl.when(home)
+        def _():
+            def step(i, carry):
+                xx = nearest(i)
+                for h in both:
+                    arrived(down, xx, h)
+
+                    @pl.when(i % 2 == 0)
+                    def _():
+                        onward(xx, h, 0).start()
+
+                    to_core(down, xx, h).start()
+                    arrived(up, xx, h)
+
+                    @pl.when(i % 2 == 1)
+                    def _():
+                        onward(xx, h, 1).start()
+
+                    to_core(up, xx, h).start()
+                return carry
+
+            lax.fori_loop(0, 4, step, 0)
+
+        take(down)
+        take(up)
+
+    def last_stage():
+        @pl.when(home)
+        def _():
+            def step(i, carry):
+                xx = nearest(i)
+                for h in both:
+                    arrived(far, xx, h)
+                    to_core(far, xx, h).start()
+                return carry
+
+            lax.fori_loop(0, 4, step, 0)
+
+        take(far)
+
+    def take(yy):
+        @pl.when(jnp.logical_not(home))
+        def _():
+            def step(i, carry):
+                for h in both:
+                    arrived(yy, nearest(i), h)
+                return carry
+
+            lax.fori_loop(0, 4, step, 0)
 
     def drain():
         @pl.when(jnp.logical_not(root))
         def _():
-            hop.wait_send()
+            for hop in hops:
+                hop.wait_send()
 
         @pl.when(home)
         def _():
-            def step(xx, carry):
-                @pl.when(root)
-                def _():
-                    to_z(xx).wait_send()
-
-                to_y(xx, 0).wait_send()
-                to_y(xx, 1).wait_send()
-
-                @pl.when(xx < 2)
-                def _():
-                    onward(xx, 0).wait_send()
-
-                @pl.when(xx >= 2)
-                def _():
-                    onward(xx, 1).wait_send()
+            def step(i, carry):
+                xx = nearest(i)
+
+                for h in both:
+
+                    @pl.when(root)
+                    def _():
+                        to_z(xx, h).wait_send()
+
+                    to_y(xx, h, 0).wait_send()
+                    to_y(xx, h, 1).wait_send()
+
+                    @pl.when(i % 2 == 0)
+                    def _():
+                        onward(xx, h, 0).wait_send()
+
+                    @pl.when(i % 2 == 1)
+                    def _():
+                        onward(xx, h, 1).wait_send()
 
                 return carry
 
             lax.fori_loop(0, 4, step, 0)
 
             def core_step(i, carry):
-                to_core(i // 4, i % 4).wait_send()
+                for h in both:
+                    to_core(i // 4, i % 4, h).wait_send()
                 return carry
 
             lax.fori_loop(0, 16, core_step, 0)
 
-    return drain
+    return own_stage, near_stage, last_stage, drain
 
 
 def group_at(j):
@@ -263,7 +316,6 @@
     product,
     relay,
     final,
-    own_sum,
     square_out,
     square_in,
     query_send,
@@ -300,7 +352,8 @@
     blk_up, blk_far, blk_down = [((zh + i) % 4) * 4 + x for i in (1, 2, 3)]
     turn = (1.0 / math.sqrt(128)) * math.log2(math.e)
 
-    chunks_w = (pl.ds(0, width), pl.ds(width, width))
+    bounds_w = ((0, width), (width, 2 * width))
+    chunks_w = tuple(pl.ds(low, high - low) for low, high in bounds_w)
     over_z = y * 4 + (1 - zl) * 2 + core
 
     def ahead(j):
@@ -454,8 +507,9 @@
         for p in range(keys_here // 128):
             block = kv_all[part_of(r), p * 128 : (p + 1) * 128, 128:256].astype(jnp.float32)
             start = r * keys_here + p * 128
-            values_t[:, start : start + 128] = jnp.transpose(block).astype(jnp.bfloat16)
-
+            values_t[0:128, start : start + 128] = jnp.transpose(block).astype(jnp.bfloat16)
+
+    values_t[128:144, :] = jnp.ones((16, values_t.shape[1]), jnp.bfloat16)
     turn_values(0)
     page_piece(1, 2, sibling).wait_recv()
     turn_values(1)
@@ -478,14 +532,13 @@
             top = jnp.maximum(top, folded + hide[j, part, page : page + 1, :])
         return top
 
-    def weigh_chunk(c, j, a, top, total, weighted):
+    def weigh_chunk(c, j, a, top, weighted):
         part = part_of(2 * a + c // per_core)
         for p in range(chunk // 128):
             page = (c % per_core) * (chunk // 128) + p
             rows = slice(c * chunk + p * 128, c * chunk + (p + 1) * 128)
             level = top - 4.0 * hide[j, part, page : page + 1, :]
             weights = jnp.exp2((scores[rows, :] - level) * turn)
-            total = total + fold(weights, jnp.add)
             probs[rows, :] = weights.astype(jnp.bfloat16)
         columns = pl.ds(pl.multiple_of(a * 2 * keys_here + c * chunk, chunk), chunk)
         product_here = jnp.dot(
@@ -493,7 +546,7 @@
             probs[c * chunk : (c + 1) * chunk, :],
             preferred_element_type=jnp.float32,
         )
-        return total, product_here if weighted is None else weighted + product_here
+        return product_here if weighted is None else weighted + product_here
 
     first_row = lax.broadcasted_iota(jnp.int32, (8, rows_all), 0) == 0
 
@@ -519,7 +572,6 @@
         return jnp.where(u < 4, u, later), jnp.where(u < 4, 0, 1)
 
     low = jnp.full((8, rows_all), NEGATIVE, jnp.float32)
-    zero = jnp.zeros((8, rows_all), jnp.float32)
 
     relays = [weight_relays(w_ref, w_all, w_send, w_recv, q, chunks_w[q]) for q in range(2)]
 
@@ -529,14 +581,14 @@
             weight_wait(w_ref, w_all, w_send, w_recv, q, chunks_w[q], source, part)
             copy.start()
 
-    def second_weights():
+    def more_weights():
         for copy in sends[1]:
             copy.start()
 
     def unit_step(u, carry):
         j, a = unit(u)
 
-        @pl.when(u == 7)
+        @pl.when(u == 4)
         def _():
             relay_chunk(0)
 
@@ -557,13 +609,13 @@
             page_piece(3, 2, sibling).wait_recv()
             turn_values(3)
 
-        top, total, weighted = low, zero, None
+        top, weighted = low, None
         for c in range(chunks):
             top = score_chunk(c, j, a, top)
         top = last_fold(top, jnp.max)
         for c in range(chunks):
-            total, weighted = weigh_chunk(c, j, a, top, total, weighted)
-        total = last_fold(total, jnp.sum)
+            weighted = weigh_chunk(c, j, a, top, weighted)
+        total, weighted = weighted[128:129], weighted[0:128]
 
         @pl.when(u < 4)
         def _():
@@ -624,9 +676,110 @@
     u_ref[tokens : tokens + 16, 128:256] = jnp.broadcast_to(below, (16, 128))
     u_ref[tokens : tokens + 16, 256:features] = jnp.zeros((16, features - 256), jnp.bfloat16)
 
-    drain = spread_features(
-        u_ref, a_all, x_send, z_send, y_send, on_send, core_send, a_recv, second_weights
+    own_stage, near_stage, last_stage, drain = spread_features(
+        u_ref, a_all, x_send, z_send, y_send, on_send, core_send, a_recv, more_weights
     )
+
+    def multiply(zt, target, q):
+        first, end = bounds_w[q]
+        for start in range(first, end, 512):
+            cols = pl.ds(start, min(512, end - start))
+            total = jnp.dot(
+                a_all[zt, 0, 0:tokens, :], w_all[0, :, cols], preferred_element_type=jnp.float32
+            )
+            for xx in range(1, 4):
+                total = total + jnp.dot(
+                    a_all[zt, xx, 0:tokens, :],
+                    w_all[xx, :, cols],
+                    preferred_element_type=jnp.float32,
+                )
+            target[:, cols] = total.astype(target.dtype)
+
+    half = tokens // 2
+    top_rows, bottom_rows = pl.ds(0, half), pl.ds(half, half)
+
+    def exchange(q):
+        cols = chunks_w[q]
+
+        def piece(i, slot, rows, target, recv, to_blk):
+            source = product.at[slot, rows, cols]
+            return remote(source, target, r_send.at[i, q], recv, req, to_blk)
+
+        def landing(side, rows):
+            return final.at[side, rows, cols]
+
+        return (
+            piece(0, 2, top_rows, relay.at[0, :, cols], relay_recv.at[0, q], blk_up),
+            piece(1, 2, bottom_rows, relay.at[1, :, cols], relay_recv.at[1, q], blk_down),
+            piece(2, 1, bottom_rows, landing(0, bottom_rows), final_recv.at[0, 1, q], blk_up),
+            piece(3, 3, top_rows, landing(1, top_rows), final_recv.at[1, 0, q], blk_down),
+            piece(4, 1, top_rows, landing(0, top_rows), final_recv.at[0, 0, q], blk_up),
+            piece(5, 3, bottom_rows, landing(1, bottom_rows), final_recv.at[1, 1, q], blk_down),
+        )
+
+    exchanges = [exchange(0), exchange(1)]
+
+    def wait_weights(q):
+        for step, part in ((3, 0), (3, 1), (1, 0), (1, 1), (2, 0), (2, 1)):
+            if (step, part) not in ((3, 0), (1, 1)):
+                source = (x + step) % 4
+                weight_wait(w_ref, w_all, w_send, w_recv, q, chunks_w[q], source, part)
+
+    def add_relay(slot, rows, index, q):
+        def tile(n, carry):
+            cols = pl.ds(pl.multiple_of(n * 128, 128), 128)
+            total = product[slot, rows, cols].astype(jnp.float32) + relay[index, :, cols].astype(
+                jnp.float32
+            )
+            product[slot, rows, cols] = total.astype(jnp.bfloat16)
+            return carry
+
+        first, end = bounds_w[q]
+        lax.fori_loop(first // 128, end // 128, tile, 0)
+
+    def send_sums(q):
+        exchanges[q][0].wait_recv()
+        add_relay(1, top_rows, 0, q)
+        exchanges[q][4].start()
+        exchanges[q][1].wait_recv()
+        add_relay(3, bottom_rows, 1, q)
+        exchanges[q][5].start()
+
+    def first_step(i, carry):
+        @pl.when(i == 0)
+        def _():
+            own_stage()
+            local.wait()
+            wait_weights(0)
+
+        @pl.when(i == 1)
+        def _():
+            near_stage()
+
+        @pl.when(i == 3)
+        def _():
+            last_stage()
+
+        zt = (y + group_at(i)) % 4
+        distance = (zt + 4 - zh) % 4
+        multiply(zt, product.at[distance], 0)
+
+        @pl.when(distance == 2)
+        def _():
+            exchanges[0][0].start()
+            exchanges[0][1].start()
+
+        @pl.when(distance == 1)
+        def _():
+            exchanges[0][2].start()
+
+        @pl.when(distance == 3)
+        def _():
+            exchanges[0][3].start()
+
+        return carry
+
+    lax.fori_loop(0, 4, first_step, 0)
 
     def squares(zt, carry):
         total = jnp.zeros((8, 128), jnp.float32)
@@ -653,91 +806,18 @@
     for copy in square_copies:
         copy.start()
 
-    def multiply(zt, target, q):
-        for start, size in ((0, 512), (512, width - 512)):
-            cols = pl.ds(q * width + start, size)
-            total = jnp.dot(
-                a_all[zt, 0, 0:tokens, :], w_all[0, :, cols], preferred_element_type=jnp.float32
-            )
-            for xx in range(1, 4):
-                total = total + jnp.dot(
-                    a_all[zt, xx, 0:tokens, :],
-                    w_all[xx, :, cols],
-                    preferred_element_type=jnp.float32,
-                )
-            target[:, cols] = total.astype(target.dtype)
-
-    half = tokens // 2
-    top_rows, bottom_rows = pl.ds(0, half), pl.ds(half, half)
-
-    def exchange(q):
-        cols = chunks_w[q]
-
-        def piece(i, slot, rows, target, recv, to_blk):
-            source = product.at[slot, rows, cols]
-            return remote(source, target, r_send.at[i, q], recv, req, to_blk)
-
-        def landing(side, rows):
-            return final.at[side, rows, cols]
-
-        return (
-            piece(0, 0, top_rows, relay.at[0, :, cols], relay_recv.at[0, q], blk_up),
-            piece(1, 0, bottom_rows, relay.at[1, :, cols], relay_recv.at[1, q], blk_down),
-            piece(2, 1, bottom_rows, landing(0, bottom_rows), final_recv.at[0, 1, q], blk_up),
-            piece(3, 2, top_rows, landing(1, top_rows), final_recv.at[1, 0, q], blk_down),
-            piece(4, 1, top_rows, landing(0, top_rows), final_recv.at[0, 0, q], blk_up),
-            piece(5, 2, bottom_rows, landing(1, bottom_rows), final_recv.at[1, 1, q], blk_down),
-        )
-
-    exchanges = [exchange(0), exchange(1)]
-
-    def wait_weights(q):
-        for step, part in ((3, 0), (3, 1), (1, 0), (1, 1), (2, 0), (2, 1)):
-            if (step, part) not in ((3, 0), (1, 1)):
-                source = (x + step) % 4
-                weight_wait(w_ref, w_all, w_send, w_recv, q, chunks_w[q], source, part)
-
-    def add_relay(slot, rows, index, q):
-        def tile(n, carry):
-            cols = pl.ds(pl.multiple_of(q * width + n * 128, 128), 128)
-            total = product[slot, rows, cols].astype(jnp.float32) + relay[index, :, cols].astype(
-                jnp.float32
-            )
-            product[slot, rows, cols] = total.astype(jnp.bfloat16)
-            return carry
-
-        lax.fori_loop(0, width // 128, tile, 0)
-
-    def send_far(q):
-        wait_weights(q)
-        multiply((zh + 2) % 4, product.at[0], q)
-        exchanges[q][0].start()
-        exchanges[q][1].start()
-
-    def send_near(q):
-        multiply((zh + 1) % 4, product.at[1], q)
-        exchanges[q][2].start()
-        multiply((zh + 3) % 4, product.at[2], q)
-        exchanges[q][3].start()
-
-    def send_sums(q):
-        exchanges[q][0].wait_recv()
-        add_relay(1, top_rows, 0, q)
-        exchanges[q][4].start()
-        exchanges[q][1].wait_recv()
-        add_relay(2, bottom_rows, 1, q)
-        exchanges[q][5].start()
-
-    local.wait()
-    send_far(0)
-    send_near(0)
     relay_chunk(1)
     send_sums(0)
-    send_far(1)
-    send_near(1)
+    wait_weights(1)
+    multiply((zh + 2) % 4, product.at[2], 1)
+    exchanges[1][0].start()
+    exchanges[1][1].start()
+    multiply((zh + 1) % 4, product.at[1], 1)
+    exchanges[1][2].start()
+    multiply((zh + 3) % 4, product.at[3], 1)
+    exchanges[1][3].start()
+    multiply(zh, product.at[0], 1)
     send_sums(1)
-    multiply(zh, own_sum, 0)
-    multiply(zh, own_sum, 1)
 
     for copy in square_copies:
         copy.wait_recv()
@@ -752,7 +832,7 @@
     def finish(n, carry):
         def column_sum(start):
             cols = pl.ds(pl.multiple_of(start, 128), 128)
-            total = own_sum[:, cols] + final[0, :, cols].astype(jnp.float32)
+            total = product[0, :, cols].astype(jnp.float32) + final[0, :, cols].astype(jnp.float32)
             return (total + final[1, :, cols].astype(jnp.float32)) * scale
 
         gate, up = column_sum(n * 128), column_sum(width + n * 128)
@@ -805,7 +885,7 @@
             pltpu.VMEM((groups, 4, keys_here // 128, rows_all), f32),
             pltpu.VMEM((groups, rows_all, 128), bf16),
             pltpu.VMEM((4, keys_here, lanes), bf16),
-            pltpu.VMEM((128, 2 * keys), bf16),
+            pltpu.VMEM((144, 2 * keys), bf16),
             pltpu.VMEM((keys, rows_all), f32),
             pltpu.VMEM((keys, rows_all), bf16),
             pltpu.VMEM((groups, 128, rows_all), bf16),
@@ -817,10 +897,9 @@
             pltpu.VMEM((tokens + 16, features), bf16),
             pltpu.VMEM((4, depth, wide), bf16),
             pltpu.VMEM((4, 4, tokens + 16, features), bf16),
-            pltpu.VMEM((3, tokens, wide), bf16),
+            pltpu.VMEM((4, tokens, wide), bf16),
             pltpu.VMEM((2, tokens // 2, wide), bf16),
             pltpu.VMEM((2, tokens, wide), bf16),
-            pltpu.VMEM((tokens, wide), f32),
             pltpu.VMEM((4, 8, 128), f32),
             pltpu.VMEM((3, 8, 128), f32),
             dma((groups,)),
@@ -834,12 +913,12 @@
             dma((6, 2)),
             dma((4, 2, 2)),
             dma,
-            dma,
-            dma((4,)),
+            dma((2,)),
             dma((4, 2)),
-            dma((4,)),
-            dma((4, 4)),
-            dma((4, 4)),
+            dma((4, 2, 2)),
+            dma((4, 2)),
+            dma((4, 4, 2)),
+            dma((4, 4, 2)),
             dma((6, 2)),
             dma((2, 2)),
             dma((2, 2, 2)),

time: 105 us -> 102 us (0.971)
  the two profiles are of different devices: /device:TPU:7 before, /device:TPU:20 now
where the time goes in v1:
time: 102 us; the launch traced here: 101 us
  Pallas kernels  94.7 us (93%)
  local copies, waits for them, and re-layouts  6.06 us (6%)
    pallas_call x1, Pallas kernels, layer(): pl.pallas_call(layer_kernel, out_shape=(jax.ShapeDtypeStruct((tokens, wid...  94.7 us
    unnamed x3, local copies, waits for them, and re-layouts  6.06 us

profile of v1, /device:TPU:20, one launch (start us, length us, event | category | flops | bytes accessed | tf_op | source)
XLA Modules:
  0.0 101.4 jit_solution(565515450497838734)
XLA Ops:
  0.6 3.0 %copy.12 = bf16[64,8,2,896]{3,1,2,0:T(8,128)(2,1)} copy(bf16[64,8,2,896]{3,2,1,0:T(2,128)(2,1)} %bitcast.8) | data formatting | bytes 3670016
  3.7 94.7 %layer.1 = (bf16[128,896]{1,0:T(8,128)(2,1)}, bf16[128,128]{1,0:T(8,128)(2,1)}) custom-call(s32[4,16]{1,0:T(4,128)} %bitcast.9, s32[16]{0:T(128)} %counts_ref.1, bf16[128,512]{1,0:T(8,128)(2,1)} %q_ref.1, f32[1,128]{1,0:T(1,128)} %constant.2.clone.inverse_ref, s32[1,128]{1,0:T(1,128)} %bitcast.11, bf16[128,8,256]{2,1,0:T(8,128)(2,1)} %suffix_ref.1, ...), custom_call_target="tpu_custom_call" | custom-call | tf_op jit(solution)/shard_map/layer/pallas_call | solution.py:871
  98.3 1.6 %copy.15 = bf16[128,896]{1,0:T(8,128)(2,1)} copy(bf16[128,896]{1,0:T(8,128)(2,1)} %get-tuple-element.4) | data formatting | bytes 458752
  100.0 1.4 %copy.16 = bf16[128,128]{1,0:T(8,128)(2,1)} copy(bf16[128,128]{1,0:T(8,128)(2,1)} %get-tuple-element.5) | data formatting | bytes 65536

commit v2 on v1

--- a/solution.py
+++ b/solution.py
@@ -926,7 +926,9 @@
             dma((3,)),
             dma((4,)),
         ],
-        compiler_params=pltpu.CompilerParams(collective_id=1, has_side_effects=True),
+        compiler_params=pltpu.CompilerParams(
+            collective_id=1, has_side_effects=True, vmem_limit_bytes=48 * 2**20
+        ),
         name="layer",
     )(
         lengths,

time: 102 us -> 97.5 us (0.956)
  local copies, waits for them, and re-layouts: 6.06 us -> 3.18 us
  Pallas kernels: 94.7 us -> 93.3 us
    unnamed x3 -> x19, local copies, waits for them, and re-layouts: 6.06 us -> 3.18 us
    pallas_call x1, Pallas kernels: 94.7 us -> 93.3 us  [layer(): pl.pallas_call(layer_kernel, out_shape=(jax.ShapeDtypeStruct((tokens, wid...]
where the time goes in v2:
time: 97.5 us; the launch traced here: 97.3 us
  Pallas kernels  93.3 us (96%)
  local copies, waits for them, and re-layouts  3.18 us (3%)
    pallas_call x1, Pallas kernels, layer(): pl.pallas_call(layer_kernel, out_shape=(jax.ShapeDtypeStruct((tokens, wid...  93.3 us
    unnamed x19, local copies, waits for them, and re-layouts  3.18 us

profile of v2, /device:TPU:20, one launch (start us, length us, event | category | flops | bytes accessed | tf_op | source)
XLA Modules:
  0.0 97.3 jit_solution(4083165938830080632)
XLA Ops:
  0.6 0.0 copy-start
  0.6 0.0 copy-start.1
  0.7 0.0 copy-start.2
  0.7 0.0 copy-start.3
  0.7 0.0 copy-start.4
  0.7 0.0 copy-start.5
  0.7 0.0 copy-start.6
  0.7 0.0 copy-start.7
  0.7 1.8 %copy.12 = bf16[64,8,2,896]{3,1,2,0:T(8,128)(2,1)S(1)} copy(bf16[64,8,2,896]{3,2,1,0:T(2,128)(2,1)} %bitcast.11) | data formatting | bytes 3670016
  2.6 0.0 copy-done
  2.6 0.0 copy-done.1
  2.6 0.0 copy-done.2
  2.6 0.0 copy-done.3
  2.6 0.0 copy-done.4
  2.6 0.0 copy-done.5
  2.6 0.0 copy-done.6
  2.6 0.0 copy-done.7
  2.6 93.3 %layer.1 = (bf16[128,896]{1,0:T(8,128)(2,1)S(1)}, bf16[128,128]{1,0:T(8,128)(2,1)S(1)}) custom-call(s32[4,16]{1,0:T(4,128)S(1)} %bitcast.7, s32[16]{0:T(128)S(1)} %copy-done.5, bf16[128,512]{1,0:T(8,128)(2,1)S(1)} %copy-done.1, f32[1,128]{1,0:T(1,128)S(1)} %copy-done.7, s32[1,128]{1,0:T(1,128)S(1)} %bitcast.9, bf16[128,8,256]{2,1,0:T(8,128)(2,1)S(1)} %copy-done, ...), custom_call_target="tpu_custom_call" | custom-call | tf_op jit(solution)/shard_map/layer/pallas_call | solution.py:871
  95.9 0.7 copy.15
  96.6 0.6 copy.16
Async XLA Ops:
  0.6 1.9 %copy-start = (bf16[128,8,256]{2,1,0:T(8,128)(2,1)S(1)}, bf16[128,8,256]{2,1,0:T(8,128)(2,1)}, u32[]{:S(2)}) copy-start(bf16[128,8,256]{2,1,0:T(8,128)(2,1)} %suffix_ref.1) | copy-start | bytes 1572868
  0.6 1.9 %copy-start.1 = (bf16[128,512]{1,0:T(8,128)(2,1)S(1)}, bf16[128,512]{1,0:T(8,128)(2,1)}, u32[]{:S(2)}) copy-start(bf16[128,512]{1,0:T(8,128)(2,1)} %q_ref.1) | copy-start | bytes 393220
  0.7 1.9 %copy-start.2 = (bf16[128,512]{1,0:T(8,128)(2,1)S(1)}, bf16[128,512]{1,0:T(8,128)(2,1)}, u32[]{:S(2)}) copy-start(bf16[128,512]{1,0:T(8,128)(2,1)} %residual_ref.1) | copy-start | bytes 393220
  0.7 1.9 %copy-start.3 = (s32[16,4]{0,1:T(4,128)S(1)}, s32[16,4]{0,1:T(4,128)}, u32[]{:S(2)}) copy-start(s32[16,4]{0,1:T(4,128)} %param.17) | copy-start | bytes 772
  0.7 1.9 %copy-start.4 = (f32[512]{0:T(512)S(1)}, f32[512]{0:T(512)}, u32[]{:S(2)}) copy-start(f32[512]{0:T(512)} %param.13) | copy-start | bytes 6148
  0.7 1.9 %copy-start.5 = (s32[16]{0:T(128)S(1)}, s32[16]{0:T(128)}, u32[]{:S(2)}) copy-start(s32[16]{0:T(128)} %counts_ref.1) | copy-start | bytes 196
  0.7 1.9 %copy-start.6 = (s32[128]{0:T(128)S(1)}, s32[128]{0:T(128)}, u32[]{:S(2)}) copy-start(s32[128]{0:T(128)} %param.16) | copy-start | bytes 1540
  0.7 1.9 %copy-start.7 = (f32[1,128]{1,0:T(1,128)S(1)}, f32[1,128]{1,0:T(1,128)}, u32[]{:S(2)}) copy-start(f32[1,128]{1,0:T(1,128)} %constant.2.clone.inverse_ref) | copy-start | bytes 1540

commit v3 on v2

--- a/solution.py
+++ b/solution.py
@@ -316,6 +316,7 @@
     product,
     relay,
     final,
+    gate_kept,
     square_out,
     square_in,
     query_send,
@@ -829,21 +830,26 @@
     square_sum = jnp.sum(jnp.where(diagonal, spread, 0.0), 1, keepdims=True)
     scale = jnp.broadcast_to(lax.rsqrt(square_sum / D + EPSILON), (tokens, 128))
 
-    def finish(n, carry):
-        def column_sum(start):
-            cols = pl.ds(pl.multiple_of(start, 128), 128)
-            total = product[0, :, cols].astype(jnp.float32) + final[0, :, cols].astype(jnp.float32)
-            return (total + final[1, :, cols].astype(jnp.float32)) * scale
-
-        gate, up = column_sum(n * 128), column_sum(width + n * 128)
-        value = gate / (1.0 + jnp.exp(-gate)) * up
-        hidden_ref[:, pl.ds(pl.multiple_of(n * 128, 128), 128)] = value.astype(jnp.bfloat16)
+    def column_sum(start):
+        cols = pl.ds(pl.multiple_of(start, 128), 128)
+        total = product[0, :, cols].astype(jnp.float32) + final[0, :, cols].astype(jnp.float32)
+        return (total + final[1, :, cols].astype(jnp.float32)) * scale
+
+    def finish_gate(n, carry):
+        gate = column_sum(n * 128)
+        gate_kept[:, pl.ds(pl.multiple_of(n * 128, 128), 128)] = gate / (1.0 + jnp.exp(-gate))
         return carry
 
-    for q in range(2):
+    def finish_up(n, carry):
+        cols = pl.ds(pl.multiple_of(n * 128, 128), 128)
+        value = gate_kept[:, cols] * column_sum(width + n * 128)
+        hidden_ref[:, cols] = value.astype(jnp.bfloat16)
+        return carry
+
+    for q, finish in enumerate((finish_gate, finish_up)):
         for copy in exchanges[q][2:]:
             copy.wait_recv()
-    lax.fori_loop(0, width // 128, finish, 0)
+        lax.fori_loop(0, width // 128, finish, 0)
 
     for copy in sends[0] + sends[1] + relays[0] + relays[1] + square_copies:
         copy.wait_send()
@@ -900,6 +906,7 @@
             pltpu.VMEM((4, tokens, wide), bf16),
             pltpu.VMEM((2, tokens // 2, wide), bf16),
             pltpu.VMEM((2, tokens, wide), bf16),
+            pltpu.VMEM((tokens, wide // 2), f32),
             pltpu.VMEM((4, 8, 128), f32),
             pltpu.VMEM((3, 8, 128), f32),
             dma((groups,)),

time: 97.5 us -> 97.3 us (level)
  no operation moved by 1% of the time
where the time goes in v3:
time: 97.3 us; the launch traced here: 97 us
  Pallas kernels  93.1 us (96%)
  local copies, waits for them, and re-layouts  3.18 us (3%)
    pallas_call x1, Pallas kernels, layer(): pl.pallas_call(layer_kernel, out_shape=(jax.ShapeDtypeStruct((tokens, wid...  93.1 us
    unnamed x19, local copies, waits for them, and re-layouts  3.18 us

profile of v3, /device:TPU:20, one launch (start us, length us, event | category | flops | bytes accessed | tf_op | source)
XLA Modules:
  0.0 97.0 jit_solution(992321528408932841)
XLA Ops:
  0.6 0.0 copy-start
  0.6 0.0 copy-start.1
  0.7 0.0 copy-start.2
  0.7 0.0 copy-start.3
  0.7 0.0 copy-start.4
  0.7 0.0 copy-start.5
  0.7 0.0 copy-start.6
  0.7 0.0 copy-start.7
  0.7 1.8 %copy.12 = bf16[64,8,2,896]{3,1,2,0:T(8,128)(2,1)S(1)} copy(bf16[64,8,2,896]{3,2,1,0:T(2,128)(2,1)} %bitcast.11) | data formatting | bytes 3670016
  2.6 0.0 copy-done
  2.6 0.0 copy-done.1
  2.6 0.0 copy-done.2
  2.6 0.0 copy-done.3
  2.6 0.0 copy-done.4
  2.6 0.0 copy-done.5
  2.6 0.0 copy-done.6
  2.6 0.0 copy-done.7
  2.6 93.1 %layer.1 = (bf16[128,896]{1,0:T(8,128)(2,1)S(1)}, bf16[128,128]{1,0:T(8,128)(2,1)S(1)}) custom-call(s32[4,16]{1,0:T(4,128)S(1)} %bitcast.7, s32[16]{0:T(128)S(1)} %copy-done.5, bf16[128,512]{1,0:T(8,128)(2,1)S(1)} %copy-done.1, f32[1,128]{1,0:T(1,128)S(1)} %copy-done.7, s32[1,128]{1,0:T(1,128)S(1)} %bitcast.9, bf16[128,8,256]{2,1,0:T(8,128)(2,1)S(1)} %copy-done, ...), custom_call_target="tpu_custom_call" | custom-call | tf_op jit(solution)/shard_map/layer/pallas_call | solution.py:877
  95.7 0.7 copy.15
  96.4 0.6 copy.16
Async XLA Ops:
  0.6 1.9 %copy-start = (bf16[128,8,256]{2,1,0:T(8,128)(2,1)S(1)}, bf16[128,8,256]{2,1,0:T(8,128)(2,1)}, u32[]{:S(2)}) copy-start(bf16[128,8,256]{2,1,0:T(8,128)(2,1)} %suffix_ref.1) | copy-start | bytes 1572868
  0.6 1.9 %copy-start.1 = (bf16[128,512]{1,0:T(8,128)(2,1)S(1)}, bf16[128,512]{1,0:T(8,128)(2,1)}, u32[]{:S(2)}) copy-start(bf16[128,512]{1,0:T(8,128)(2,1)} %q_ref.1) | copy-start | bytes 393220
  0.7 1.9 %copy-start.2 = (bf16[128,512]{1,0:T(8,128)(2,1)S(1)}, bf16[128,512]{1,0:T(8,128)(2,1)}, u32[]{:S(2)}) copy-start(bf16[128,512]{1,0:T(8,128)(2,1)} %residual_ref.1) | copy-start | bytes 393220
  0.7 1.9 %copy-start.3 = (s32[16,4]{0,1:T(4,128)S(1)}, s32[16,4]{0,1:T(4,128)}, u32[]{:S(2)}) copy-start(s32[16,4]{0,1:T(4,128)} %param.17) | copy-start | bytes 772
  0.7 1.9 %copy-start.4 = (f32[512]{0:T(512)S(1)}, f32[512]{0:T(512)}, u32[]{:S(2)}) copy-start(f32[512]{0:T(512)} %param.13) | copy-start | bytes 6148
  0.7 1.9 %copy-start.5 = (s32[16]{0:T(128)S(1)}, s32[16]{0:T(128)}, u32[]{:S(2)}) copy-start(s32[16]{0:T(128)} %counts_ref.1) | copy-start | bytes 196
  0.7 1.9 %copy-start.6 = (s32[128]{0:T(128)S(1)}, s32[128]{0:T(128)}, u32[]{:S(2)}) copy-start(s32[128]{0:T(128)} %param.16) | copy-start | bytes 1540
  0.7 1.9 %copy-start.7 = (f32[1,128]{1,0:T(1,128)S(1)}, f32[1,128]{1,0:T(1,128)}, u32[]{:S(2)}) copy-start(f32[1,128]{1,0:T(1,128)} %constant.2.clone.inverse_ref) | copy-start | bytes 1540
